TPU v7x, 256 devices: a whole 4x4x8 slice. The times are simulated.
256 devices in a mesh: seq: 32 (over z_lo, x, core), tp: 8 (over y, z_hi).
Axes of the slice: x: 4, y: 4, z: 8 (z_hi: 2, z_lo: 4; z = z_hi * 4 + z_lo), core: 2. Of those that a mesh axis runs over, the one named last changes fastest.
Arguments:
- hidden: bfloat16 [8192, 7168], P('seq', 'tp'), may hold values from -6 to 6
- norm_gain: bfloat16 [7168], replicated, may hold values from 0.5 to 1.5
- w_query: bfloat16 [7168, 4096], P(None, 'tp'), may hold values from -0.0625 to 0.0625
- w_key: bfloat16 [7168, 1024], P(None, 'tp'), may hold values from -0.0625 to 0.0625
- w_value: bfloat16 [7168, 1024], P(None, 'tp'), may hold values from -0.0625 to 0.0625
- prefix_keys: bfloat16 [8192, 1024], P('seq', 'tp'), may hold values from -64 to 64
- prefix_values: bfloat16 [8192, 1024], P('seq', 'tp'), may hold values from -6 to 6
- page_prefix: int32 [64], replicated, may hold values from 0 to 3, as said below
- request_prefix: int32 [32], replicated, may hold values from 0 to 3
- suffix_lengths: int32 [32], replicated, may hold values from 1 to 1024, 8192 in all
- row_order: int32 [8192], replicated, may hold values from 0 to 8191, as said below
Outputs:
- attended: bfloat16 [8192, 4096], P('seq', 'tp')
- suffix_keys: bfloat16 [8192, 1024], P('seq', 'tp')
- suffix_values: bfloat16 [8192, 1024], P('seq', 'tp')
Inputs may be any that keep to these rules, and one draw needn't show every extreme that they name: `page_prefix`: each of the 4 prefixes owns exactly 16 pages. `suffix_lengths`: the lengths sum to 8192; the longest is exactly 1024. `row_order`: a permutation of 0 to 8191 made of aligned runs of 128 consecutive values.
All inputs are finite; a program needn't handle non-finite values.
Results may differ from a plain program's by a relative error of at most 0.0075.
The roundings to bfloat16 on the way count: a program that leaves them out, or rounds other values in their place, can miss the bound.
Values may be sent and summed in bfloat16 or wider, within the bound.
A program may use at most 128 MiB of HBM per device.

v0:
```python
import math
import jax
import jax.numpy as jnp
from jax import lax
from jax.sharding import PartitionSpec as P

HEAD = 128
PAGE = 128
PREFIXES = 4
ROPE_BASE = 5000000.0


def rotate(tensor_in, positions):
    head_dim = tensor_in.shape[-1]
    half_dim = head_dim // 2
    frequency = ROPE_BASE ** (-(jnp.arange(half_dim, dtype=jnp.float32) * 2.0 / head_dim))
    angles = positions.astype(jnp.float32)[:, None] * frequency[None, :]
    cosine = jnp.cos(angles)[:, None, :]
    sine_part = jnp.sin(angles)[:, None, :]
    first_half = tensor_in[..., :half_dim]
    second_half = tensor_in[..., half_dim:]
    return jnp.concatenate(
        [
            first_half * cosine - second_half * sine_part,
            second_half * cosine + first_half * sine_part,
        ],
        axis=-1,
    )


def locate(row_order, suffix_lengths, request_prefix):
    end_rows = jnp.cumsum(suffix_lengths)
    starts = end_rows - suffix_lengths
    numbers = jnp.arange(suffix_lengths.shape[0], dtype=jnp.int32)
    request = jnp.sum((row_order[:, None] >= end_rows[None, :]).astype(jnp.int32), axis=1)
    chosen = request[:, None] == numbers[None, :]
    position = row_order - jnp.sum(jnp.where(chosen, starts[None, :], 0), axis=1)
    wanted = jnp.sum(jnp.where(chosen, request_prefix[None, :], 0), axis=1)
    return (request, position, wanted)


def body(
    hidden,
    norm_gain,
    w_query,
    w_key,
    w_value,
    prefix_keys,
    prefix_values,
    page_prefix,
    request_prefix,
    suffix_lengths,
    row_order,
):
    gathered = lax.all_gather(hidden, "tp", axis=1, tiled=True)
    local_rows = gathered.shape[0]
    hidden_f = gathered.astype(jnp.float32)
    mean_sq = jnp.mean(hidden_f * hidden_f, axis=1, keepdims=True)
    normed = (
        hidden_f * lax.rsqrt(mean_sq + 1e-05) * norm_gain.astype(jnp.float32)[None, :]
    ).astype(jnp.bfloat16)
    request_all, position_all, wanted_all = locate(row_order, suffix_lengths, request_prefix)
    offset = lax.axis_index("seq") * local_rows
    request = lax.dynamic_slice_in_dim(request_all, offset, local_rows)
    position = lax.dynamic_slice_in_dim(position_all, offset, local_rows)
    wanted = lax.dynamic_slice_in_dim(wanted_all, offset, local_rows)
    prefix_len = page_prefix.shape[0] * PAGE // PREFIXES
    rope_at = prefix_len + position
    q_heads = w_query.shape[1] // HEAD
    kv_heads = w_key.shape[1] // HEAD
    group_size = q_heads // kv_heads
    queries = rotate(
        jnp.dot(normed, w_query, preferred_element_type=jnp.float32).reshape(
            local_rows, q_heads, HEAD
        ),
        rope_at,
    ).astype(jnp.bfloat16)
    queries = queries.reshape(local_rows, kv_heads, group_size, HEAD)
    new_keys = rotate(
        jnp.dot(normed, w_key, preferred_element_type=jnp.float32).reshape(
            local_rows, kv_heads, HEAD
        ),
        rope_at,
    ).astype(jnp.bfloat16)
    new_keys = new_keys.reshape(local_rows, kv_heads * HEAD)
    new_values = jnp.dot(normed, w_value, preferred_element_type=jnp.float32).astype(jnp.bfloat16)
    row_pages = jnp.repeat(page_prefix, PAGE)
    score_scale = 1.0 / math.sqrt(HEAD)
    initial = (
        jnp.full((kv_heads, local_rows, group_size), -1e30, jnp.float32),
        jnp.zeros((kv_heads, local_rows, group_size), jnp.float32),
        jnp.zeros((kv_heads, local_rows, group_size, HEAD), jnp.float32),
    )

    def attend(state, key_rows, value_rows, visible):
        row_count = key_rows.shape[0]
        block_width = math.gcd(row_count, 512)
        block_count = row_count // block_width
        key_blocks = key_rows.reshape(block_count, block_width, kv_heads, HEAD)
        value_blocks = value_rows.reshape(block_count, block_width, kv_heads, HEAD)
        mask_blocks = visible.reshape(local_rows, block_count, block_width).transpose(1, 0, 2)

        def step(carry_in, inputs):
            run_max, run_sum, run_acc = carry_in
            key_block, value_block, mask_block = inputs
            scores = (
                jnp.einsum("tngd,knd->ntgk", queries, key_block, preferred_element_type=jnp.float32)
                * score_scale
            )
            seen = mask_block[None, :, None, :]
            new_max = jnp.maximum(run_max, jnp.max(jnp.where(seen, scores, -1e30), axis=-1))
            weights = jnp.where(seen, jnp.exp(scores - new_max[..., None]), 0.0)
            fade = jnp.exp(run_max - new_max)
            run_sum = run_sum * fade + jnp.sum(weights, axis=-1)
            run_acc = run_acc * fade[..., None] + jnp.einsum(
                "ntgk,knd->ntgd",
                weights.astype(jnp.bfloat16),
                value_block,
                preferred_element_type=jnp.float32,
            )
            return ((new_max, run_sum, run_acc), None)

        result, unused = lax.scan(step, state, (key_blocks, value_blocks, mask_blocks))
        return result

    key_rows = lax.all_gather(prefix_keys, "seq", axis=0, tiled=True)
    value_rows = lax.all_gather(prefix_values, "seq", axis=0, tiled=True)
    visible = wanted[:, None] == row_pages[None, :]
    state = attend(initial, key_rows, value_rows, visible)
    key_rows = lax.all_gather(new_keys, "seq", axis=0, tiled=True)
    value_rows = lax.all_gather(new_values, "seq", axis=0, tiled=True)
    visible = (request[:, None] == request_all[None, :]) & (
        position_all[None, :] <= position[:, None]
    )
    state = attend(state, key_rows, value_rows, visible)
    run_max, run_sum, run_acc = state
    attended = (
        (run_acc / run_sum[..., None])
        .transpose(1, 0, 2, 3)
        .reshape(local_rows, q_heads * HEAD)
        .astype(jnp.bfloat16)
    )
    return (attended, new_keys, new_values)


def solution(mesh):
    return jax.shard_map(
        body,
        mesh=mesh,
        in_specs=(
            P("seq", "tp"),
            P(),
            P(None, "tp"),
            P(None, "tp"),
            P(None, "tp"),
            P("seq", "tp"),
            P("seq", "tp"),
            P(),
            P(),
            P(),
            P(),
        ),
        out_specs=(P("seq", "tp"), P("seq", "tp"), P("seq", "tp")),
        check_vma=False,
    )
```

profile of v0, /device:TPU:1, one launch (start us, length us, event | category | flops | bytes accessed | tf_op | source)
XLA Modules:
  0.0 437.9 jit_solution(14165126439068676029)
XLA Ops:
  14.6 98.3 %all-gather.8.cloned.1.call-done = bf16[256,7168]{1,0:T(8,128)(2,1)} async-done(((bf16[256,896]{1,0:T(8,128)(2,1)}), bf16[256,7168]{1,0:T(8,128)(2,1)}) %all-gather.8.cloned.1.call-update) | async-done | bytes 3670032 | tf_op jit(solution)/shard_map/all_gather | solution.py:55
  112.9 3.0 fusion.44
  119.7 2.8 broadcast_compare_fusion
  122.5 4.7 %compare_and_fusion = pred[16,256,512]{1,2,0:T(8,128)(4,1)} fusion(s32[256]{0:T(256)S(1)} %get-tuple-element.194, s32[16,512]{1,0:T(8,128)S(1)} %le.17, s32[16,512]{1,0:T(8,128)S(1)} %eq.52, s32[256]{0:T(256)S(1)} %dynamic_slice.31), kind=kLoop, calls=%fused_computation.60 | loop fusion | flops 6291456 | bytes 2164736 | tf_op jit(solution)/shard_map/and | solution.py:132
  127.2 6.0 %fusion.61 = f32[256,512]{1,0:T(8,128)} fusion(bf16[7168,512]{1,0:T(8,128)(2,1)} %param.17, bf16[256,7168]{1,0:T(8,128)(2,1)S(1)} %copy-done.3, f32[7168]{0:T(1024)S(1)} %convert_element_type.47, f32[256]{0:T(256)S(1)} %add_rsqrt_fusion), kind=kOutput, calls=%fused_computation.97 | convolution fusion | flops 1886388224 | bytes 11564032 | tf_op jit(solution)/shard_map/dot_general | solution.py:73
  136.5 3.5 convolution_convert_fusion
  140.0 30.5 %all-gather.6.cloned.1.call-done = bf16[8192,128]{1,0:T(8,128)(2,1)} async-done(((bf16[256,128]{1,0:T(8,128)(2,1)}), bf16[8192,128]{1,0:T(8,128)(2,1)}) %all-gather.6.cloned.1.call-update) | async-done | bytes 2097168 | tf_op jit(solution)/shard_map/all_gather | solution.py:126
  170.4 60.9 %all-gather.10.cloned.1.call-done = bf16[8192,128]{1,0:T(8,128)(2,1)} async-done(((bf16[256,128]{1,0:T(8,128)(2,1)}), bf16[8192,128]{1,0:T(8,128)(2,1)}) %all-gather.10.cloned.1.call-update) | async-done | bytes 2097168 | tf_op jit(solution)/shard_map/all_gather | solution.py:127
  231.4 107.4 %while.30 = (s32[]{:T(128)}, f32[1,256,4]{1,2,0:T(4,128)S(1)}, f32[1,256,4]{1,2,0:T(4,128)S(1)}, f32[1,256,4,128]{3,1,2,0:T(8,128)S(1)}, pred[16,256,512]{1,2,0:...) while((s32[]{:T(128)}, f32[1,256,4]{1,2,0:T(4,128)S(1)}, ...), condition=%wide.region_8.9_spmd.clone, body=%wide.region_5.8_spmd.clone.sunk | while | flops 274601984 | bytes 16974992 | solution.py:123
  232.3 2.7 fusion.87
  245.7 2.7 fusion.87
  252.4 2.7 fusion.87
  259.1 2.7 fusion.87
  265.8 2.7 fusion.87
  272.6 2.7 fusion.87
  279.3 2.7 fusion.87
  292.7 2.7 fusion.87
  306.1 2.7 fusion.87
  312.8 2.7 fusion.87
  319.5 2.7 fusion.87
  333.0 2.7 fusion.87
  339.5 4.1 copy.43
  343.6 14.1 %all-gather.14.cloned.1.call-done = bf16[8192,128]{1,0:T(8,128)(2,1)} async-done(((bf16[256,128]{1,0:T(8,128)(2,1)}), bf16[8192,128]{1,0:T(8,128)(2,1)}) %all-gather.14.cloned.1.call-update) | async-done | bytes 2097168 | tf_op jit(solution)/shard_map/all_gather | solution.py:131
  357.6 72.6 %while.29 = (s32[]{:T(128)}, f32[1,256,4]{1,2,0:T(4,128)S(1)}, f32[1,256,4]{1,2,0:T(4,128)S(1)}, f32[1,256,4,128]{3,1,2,0:T(8,128)S(1)}, pred[16,256,512]{1,2,0:...) while((s32[]{:T(128)}, f32[1,256,4]{1,2,0:T(4,128)S(1)}, ...), condition=%wide.region_12.13_spmd, body=%wide.region_9.12_spmd.sunk | while | flops 274467840 | bytes 8586337 | solution.py:123
  (300 shorter events, 162.3 us)
Async XLA Ops:
  7.2 108.7 %copy-start = (bf16[7168,128]{1,0:T(8,128)(2,1)S(1)}, bf16[7168,128]{1,0:T(8,128)(2,1)}, u32[]{:S(2)}) copy-start(bf16[7168,128]{1,0:T(8,128)(2,1)} %param.18) | copy-start | bytes 5505028
  7.2 105.7 %all-gather.8.cloned.1.call-start = ((), (), s32[]{:S(2)}) async-start(), calls=%async_computation.1 | async-start | bytes 4128768 | tf_op jit(solution)/shard_map/all_gather | solution.py:55
  7.9 162.5 %all-gather.6.cloned.1.call-start = ((), (), s32[]{:S(2)}) async-start(), calls=%async_computation | async-start | bytes 2162688 | tf_op jit(solution)/shard_map/all_gather | solution.py:126
  8.7 222.7 %all-gather.10.cloned.1.call-start = ((), (), s32[]{:S(2)}) async-start(), calls=%async_computation.2 | async-start | bytes 2162688 | tf_op jit(solution)/shard_map/all_gather | solution.py:127
  9.4 330.1 %all-gather.12.cloned.1.call-start = ((), (), s32[]{:S(2)}) async-start(), calls=%async_computation.3 | async-start | bytes 2162688 | tf_op jit(solution)/shard_map/all_gather | solution.py:130
  112.9 3.1 copy-start.2
  116.0 3.0 copy-start.6
  118.6 239.1 %all-gather.14.cloned.1.call-start = ((), (), s32[]{:S(2)}) async-start(), calls=%async_computation.4 | async-start | bytes 2162688 | tf_op jit(solution)/shard_map/all_gather | solution.py:131
  119.7 7.5 %copy-start.3 = (bf16[256,7168]{1,0:T(8,128)(2,1)S(1)}, bf16[256,7168]{1,0:T(8,128)(2,1)}, u32[]{:S(2)}) copy-start(bf16[256,7168]{1,0:T(8,128)(2,1)} %all-gather.8.cloned.1.call-done) | copy-start | bytes 11010052
  231.4 107.4 %copy-start.5 = (bf16[256,128]{0,1:T(8,128)(2,1)S(1)}, bf16[256,128]{0,1:T(8,128)(2,1)}, u32[]{:S(2)}) copy-start(bf16[256,128]{0,1:T(8,128)(2,1)} %pad_maximum_fusion.1) | copy-start | bytes 196612
  235.0 2.6 copy-start.1
  241.7 2.6 copy-start.1
  248.4 2.6 copy-start.1
  255.1 2.6 copy-start.1
  261.8 2.6 copy-start.1
  268.5 2.6 copy-start.1
  275.3 2.6 copy-start.1
  282.0 2.6 copy-start.1
  295.4 2.6 copy-start.1
  302.1 2.6 copy-start.1
  315.5 2.6 copy-start.1
  322.2 2.6 copy-start.1
  329.0 2.6 copy-start.1
  335.7 2.6 copy-start.1
  (3 other events, 7.2 us)
Sparse Core Ops, SparseCore 0:
  10.6 102.2 all-gather.7
  114.7 55.6 all-gather.5
  172.3 59.0 all-gather.9
  233.6 62.8 all-gather.11
  298.7 58.8 all-gather.13
where the time goes:
time: 440 us; the launch traced here: 438 us
  waiting for transfers between devices  206 us (47%)
  matrix products  144 us (33%)
  local copies, waits for them, and re-layouts  39.5 us (9%)
  other arithmetic  32.5 us (7%)
  between operations  13.9 us (3%)
    all_gather x1, waiting for transfers between devices, body(): gathered = lax.all_gather(hidden, 'tp', axis=1, tiled=True)  98.3 us
    dot_general x32, matrix products, step(): jnp.einsum('ntgk,knd->ntgd', weights.astype(jnp.bfloat16), value_block, p...  67.7 us
    dot_general x32, matrix products, step(): jnp.einsum('tngd,knd->ntgk', queries, key_block, preferred_element_type=j...  65.6 us
    all_gather x1, waiting for transfers between devices, body(): value_rows = lax.all_gather(prefix_values, 'seq', axis=0, tiled=True)  60.9 us
    all_gather x1, waiting for transfers between devices, body(): key_rows = lax.all_gather(prefix_keys, 'seq', axis=0, tiled=True)  30.5 us
    broadcast_in_dim x32, local copies, waits for them, and re-layouts, step(): jnp.where(seen, scores, -1e+30)  29.4 us
    reduce_sum x32, other arithmetic, step(): run_sum = run_sum * fade + jnp.sum(weights, axis=-1)  14.8 us
    all_gather x1, waiting for transfers between devices, body(): value_rows = lax.all_gather(new_values, 'seq', axis=0, tiled=True)  14.1 us
  transfers between devices with their start and end apart: 5, of which 4 were waited for; matrix products, arithmetic and copies ran while one was open for 32% of the time, Pallas kernels for 0%

commit v1 on v0

--- a/solution.py
+++ b/solution.py
@@ -124,7 +124,9 @@
         return result
 
     key_rows = lax.all_gather(prefix_keys, "seq", axis=0, tiled=True)
-    value_rows = lax.all_gather(prefix_values, "seq", axis=0, tiled=True)
+    value_rows = jnp.concatenate(
+        lax.all_to_all(jnp.stack([prefix_values] * lax.axis_size("seq")), "seq", 0, 0), axis=0
+    )
     visible = wanted[:, None] == row_pages[None, :]
     state = attend(initial, key_rows, value_rows, visible)
     key_rows = lax.all_gather(new_keys, "seq", axis=0, tiled=True)

time: 440 us -> 393 us (0.89)
  waiting for transfers between devices: 206 us -> 152 us
  starting transfers between devices: 0.37 us -> 6.05 us
    all_gather x1 -> x0, waiting for transfers between devices: 60.9 us -> none  [body(): value_rows = lax.all_gather(prefix_values, 'seq', axis=0, tiled=True)]
    all_to_all x0 -> x1, waiting for transfers between devices: none -> 36.5 us  [body(): lax.all_to_all(jnp.stack([prefix_values] * lax.axis_size('seq')), 'seq',...]
    all_gather x1, waiting for transfers between devices: 30.5 us -> 2.14 us  [body(): key_rows = lax.all_gather(prefix_keys, 'seq', axis=0, tiled=True)]
    all_to_all x0 -> x1, starting transfers between devices: none -> 5.72 us  [body(): lax.all_to_all(jnp.stack([prefix_values] * lax.axis_size('seq')), 'seq',...]
  transfers between devices with their start and end apart: 5 -> 5, of which waited for: 4 -> 4; matrix products, arithmetic and copies ran while one was open for 32% -> 37% of each run, Pallas kernels for 0% -> 0%
where the time goes in v1:
time: 393 us; the launch traced here: 391 us
  waiting for transfers between devices  152 us (39%)
  matrix products  145 us (37%)
  local copies, waits for them, and re-layouts  39.9 us (10%)
  other arithmetic  32.3 us (8%)
  between operations  13.9 us (4%)
  starting transfers between devices  6.05 us (2%)
    all_gather x1, waiting for transfers between devices, body(): gathered = lax.all_gather(hidden, 'tp', axis=1, tiled=True)  99 us
    dot_general x32, matrix products, step(): jnp.einsum('ntgk,knd->ntgd', weights.astype(jnp.bfloat16), value_block, p...  67.7 us
    dot_general x32, matrix products, step(): jnp.einsum('tngd,knd->ntgk', queries, key_block, preferred_element_type=j...  65.4 us
    all_to_all x1, waiting for transfers between devices, body(): lax.all_to_all(jnp.stack([prefix_values] * lax.axis_size('seq')), 'seq',...  36.5 us
    broadcast_in_dim x32, local copies, waits for them, and re-layouts, step(): jnp.where(seen, scores, -1e+30)  29.4 us
    reduce_sum x32, other arithmetic, step(): run_sum = run_sum * fade + jnp.sum(weights, axis=-1)  14.8 us
    all_gather x1, waiting for transfers between devices, body(): value_rows = lax.all_gather(new_values, 'seq', axis=0, tiled=True)  13.3 us
  transfers between devices with their start and end apart: 5, of which 4 were waited for; matrix products, arithmetic and copies ran while one was open for 37% of the time, Pallas kernels for 0%

profile of v1, /device:TPU:1, one launch (start us, length us, event | category | flops | bytes accessed | tf_op | source)
XLA Modules:
  0.0 391.3 jit_solution(14127002408386061200)
XLA Ops:
  13.9 99.0 %all-gather.7.cloned.1.call-done = bf16[256,7168]{1,0:T(8,128)(2,1)} async-done(((bf16[256,896]{1,0:T(8,128)(2,1)}), bf16[256,7168]{1,0:T(8,128)(2,1)}) %all-gather.7.cloned.1.call-update) | async-done | bytes 3670032 | tf_op jit(solution)/shard_map/all_gather | solution.py:55
  112.9 3.0 fusion.44
  120.4 5.7 %all-to-all-start = ((bf16[32,256,128]{2,1,0:T(8,128)(2,1)}), bf16[32,256,128]{2,1,0:T(8,128)(2,1)}, u32[]{:S(2)}, u32[]{:S(2)}) async-start(bf16[32,256,128]{2,1,0:T(8,128)(2,1)} %stack.2), calls=%async_computation | async-start | bytes 4194304 | tf_op jit(solution)/shard_map/all_to_all | solution.py:128
  129.9 4.6 %compare_and_fusion = pred[16,256,512]{1,2,0:T(8,128)(4,1)} fusion(s32[256]{0:T(256)S(1)} %get-tuple-element.194, s32[16,512]{1,0:T(8,128)S(1)} %le.17, s32[16,512]{1,0:T(8,128)S(1)} %eq.52, s32[256]{0:T(256)S(1)} %dynamic_slice.31), kind=kLoop, calls=%fused_computation.60 | loop fusion | flops 6291456 | bytes 2164736 | tf_op jit(solution)/shard_map/and | solution.py:134
  134.5 6.0 %fusion.61 = f32[256,512]{1,0:T(8,128)} fusion(bf16[7168,512]{1,0:T(8,128)(2,1)} %param.17, bf16[256,7168]{1,0:T(8,128)(2,1)S(1)} %copy-done.3, f32[7168]{0:T(1024)S(1)} %convert_element_type.47, f32[256]{0:T(256)S(1)} %add_rsqrt_fusion), kind=kOutput, calls=%fused_computation.97 | convolution fusion | flops 1886388224 | bytes 11564032 | tf_op jit(solution)/shard_map/dot_general | solution.py:73
  141.8 4.5 %convolution_convert_fusion = bf16[256,128]{1,0:T(8,128)(2,1)} fusion(bf16[7168,128]{1,0:T(8,128)(2,1)} %param.19, bf16[256,7168]{1,0:T(8,128)(2,1)} %all-gather.7.cloned.1.call-done, f32[7168]{0:T(1024)S(1)} %convert_element_type.47, f32[256]{0:T(256)S(1)} %add_rsqrt_fusion), kind=kOutput, calls=%fused_computation.66 | convolution fusion | flops 477134848 | bytes 5600256 | tf_op jit(solution)/shard_map/dot_general | solution.py:86
  147.0 36.5 %all-to-all-done = bf16[32,256,128]{2,1,0:T(8,128)(2,1)} async-done(((bf16[32,256,128]{2,1,0:T(8,128)(2,1)}), bf16[32,256,128]{2,1,0:T(8,128)(2,1)}, u32[]{:S(2)}, u32[]{:S(2)}) %all-to-all-start) | async-done | bytes 2097184 | tf_op jit(solution)/shard_map/all_to_all | solution.py:128
  185.7 107.2 %while.30 = (s32[]{:T(128)}, f32[1,256,4]{1,2,0:T(4,128)S(1)}, f32[1,256,4]{1,2,0:T(4,128)S(1)}, f32[1,256,4,128]{3,1,2,0:T(8,128)S(1)}, pred[16,256,512]{1,2,0:...) while((s32[]{:T(128)}, f32[1,256,4]{1,2,0:T(4,128)S(1)}, ...), condition=%wide.region_8.9_spmd.clone, body=%wide.region_5.8_spmd.clone.sunk | while | flops 274601984 | bytes 16974992 | solution.py:123
  186.6 2.7 fusion.87
  193.3 2.7 fusion.87
  200.0 2.7 fusion.87
  206.7 2.7 fusion.87
  213.4 2.7 fusion.87
  220.1 2.7 fusion.87
  226.8 2.7 fusion.87
  233.5 2.7 fusion.87
  240.2 2.7 fusion.87
  246.9 2.7 fusion.87
  273.7 2.7 fusion.87
  280.3 2.7 fusion.87
  287.1 2.7 fusion.87
  293.6 4.1 %copy.43 = bf16[8192,128]{1,0:T(8,128)(2,1)} copy(bf16[8192,128]{0,1:T(8,128)(2,1)} %all-gather.9.cloned.1.call-done) | data formatting | bytes 4194304 | tf_op jit(solution)/shard_map/while | solution.py:123
  297.7 13.3 %all-gather.11.cloned.1.call-done = bf16[8192,128]{1,0:T(8,128)(2,1)} async-done(((bf16[256,128]{1,0:T(8,128)(2,1)}), bf16[8192,128]{1,0:T(8,128)(2,1)}) %all-gather.11.cloned.1.call-update) | async-done | bytes 2097168 | tf_op jit(solution)/shard_map/all_gather | solution.py:133
  311.0 72.6 %while.29 = (s32[]{:T(128)}, f32[1,256,4]{1,2,0:T(4,128)S(1)}, f32[1,256,4]{1,2,0:T(4,128)S(1)}, f32[1,256,4,128]{3,1,2,0:T(8,128)S(1)}, pred[16,256,512]{1,2,0:...) while((s32[]{:T(128)}, f32[1,256,4]{1,2,0:T(4,128)S(1)}, ...), condition=%wide.region_12.13_spmd, body=%wide.region_9.12_spmd.sunk | while | flops 274467840 | bytes 8586337 | solution.py:123
  (300 shorter events, 164.1 us)
Async XLA Ops:
  7.2 108.7 %copy-start = (bf16[7168,128]{1,0:T(8,128)(2,1)S(1)}, bf16[7168,128]{1,0:T(8,128)(2,1)}, u32[]{:S(2)}) copy-start(bf16[7168,128]{1,0:T(8,128)(2,1)} %param.18) | copy-start | bytes 5505028
  7.2 105.7 %all-gather.7.cloned.1.call-start = ((), (), s32[]{:S(2)}) async-start(), calls=%async_computation.2 | async-start | bytes 4128768 | tf_op jit(solution)/shard_map/all_gather | solution.py:55
  7.9 177.7 %all-gather.5.cloned.1.call-start = ((), (), s32[]{:S(2)}) async-start(), calls=%async_computation.1 | async-start | bytes 2162688 | tf_op jit(solution)/shard_map/all_gather | solution.py:126
  8.7 284.9 %all-gather.9.cloned.1.call-start = ((), (), s32[]{:S(2)}) async-start(), calls=%async_computation.3 | async-start | bytes 2162688 | tf_op jit(solution)/shard_map/all_gather | solution.py:132
  112.9 3.1 copy-start.2
  120.4 6.2 %copy-start.6 = (s32[64]{0:T(128)S(1)}, s32[64]{0:T(128)}, u32[]{:S(2)}) copy-start(s32[64]{0:T(128)} %param.22) | copy-start | bytes 772
  120.4 63.1 %all-to-all-start = ((bf16[32,256,128]{2,1,0:T(8,128)(2,1)}), bf16[32,256,128]{2,1,0:T(8,128)(2,1)}, u32[]{:S(2)}, u32[]{:S(2)}) async-start(bf16[32,256,128]{2,1,0:T(8,128)(2,1)} %stack.2), calls=%async_computation | async-start | bytes 4194304 | tf_op jit(solution)/shard_map/all_to_all | solution.py:128
  126.1 184.9 %all-gather.11.cloned.1.call-start = ((), (), s32[]{:S(2)}) async-start(), calls=%async_computation.4 | async-start | bytes 2162688 | tf_op jit(solution)/shard_map/all_gather | solution.py:133
  127.3 7.3 %copy-start.3 = (bf16[256,7168]{1,0:T(8,128)(2,1)S(1)}, bf16[256,7168]{1,0:T(8,128)(2,1)}, u32[]{:S(2)}) copy-start(bf16[256,7168]{1,0:T(8,128)(2,1)} %all-gather.7.cloned.1.call-done) | copy-start | bytes 11010052
  185.7 107.2 %copy-start.4 = (bf16[256,128]{0,1:T(8,128)(2,1)S(1)}, bf16[256,128]{0,1:T(8,128)(2,1)}, u32[]{:S(2)}) copy-start(bf16[256,128]{0,1:T(8,128)(2,1)} %pad_maximum_fusion.1) | copy-start | bytes 196612
  189.3 2.6 copy-start.1
  196.0 2.6 copy-start.1
  202.7 2.6 copy-start.1
  209.4 2.6 copy-start.1
  216.1 2.6 copy-start.1
  222.8 2.6 copy-start.1
  242.9 2.6 copy-start.1
  249.6 2.6 copy-start.1
  256.3 2.6 copy-start.1
  262.9 2.6 copy-start.1
  269.6 2.6 copy-start.1
  276.4 2.6 copy-start.1
  283.0 2.6 copy-start.1
  289.7 2.6 copy-start.1
  (3 other events, 7.6 us)
Sparse Core Ops, SparseCore 0:
  10.6 102.2 all-gather.6
  114.7 70.8 all-gather.4
  188.0 61.7 all-gather.8
  252.1 58.8 all-gather.10
